TPU v7x, 256 devices: a whole 4x4x8 slice. The times are simulated.
256 devices in a mesh: seq: 32 (over y, x, core), fsdp: 8 (over z).
Axes of the slice: x: 4, y: 4, z: 8, core: 2. Of those that a mesh axis runs over, the one named last changes fastest.
Arguments:
- normed_block_input: bfloat16 [8, 4096, 8192], P('fsdp', 'seq'), may hold values from -6 to 6
- stored_rotated_queries: bfloat16 [8, 4096, 4096], P('fsdp', 'seq'), may hold values from -640 to 640
- stored_rotated_keys: bfloat16 [8, 4096, 512], P('fsdp', 'seq'), may hold values from -4 to 4
- attention_output_gradient: bfloat16 [8, 4096, 4096], P('fsdp', 'seq'), may hold values from -6 to 6
- frozen_value_weight: bfloat16 [8192, 512], P('fsdp'), may hold values from -0.0625 to 0.0625
- adapter_down_weight: bfloat16 [16, 8192], replicated, may hold values from -0.0625 to 0.0625
- adapter_up_weight: bfloat16 [16, 512], replicated, may hold values from -1.5 to 1.5
- packed_document_lengths: int32 [8, 8], P('fsdp'), may hold values from 1 to 1024, 4096 in all within a row
Outputs:
- input_gradient: bfloat16 [8, 4096, 8192], P('fsdp', 'seq')
- rotated_query_gradient: bfloat16 [8, 4096, 4096], P('fsdp', 'seq')
- rotated_key_gradient: bfloat16 [8, 4096, 512], P('fsdp', 'seq')
- adapter_down_gradient: float32 [16, 8192], replicated
- adapter_up_gradient: float32 [16, 512], replicated
Inputs may be any that keep to these rules, and one draw needn't show every extreme that they name: `packed_document_lengths`: row g holds, in order, the lengths of the 8 documents packed into sequence g; they sum to 4096, and in every row the longest has exactly 1024 tokens.
All inputs are finite; a program needn't handle non-finite values.
Results may differ from a plain program's by a relative error of at most 0.0065.
Values may be sent and summed in bfloat16 or wider, within the bound.
A program may use at most 128 MiB of HBM per device.

v0:
```python
import jax
import jax.numpy as jnp
from jax import lax
from jax.sharding import PartitionSpec as P

HEAD_FEATURES = 128
QUERY_HEADS = 32
KEY_VALUE_HEADS = 4
ADAPTER_SCALE = 2.0
NEG_FILL = -1e30


def contract_trailing(left_rows, right_rows):
    return lax.dot_general(
        left_rows, right_rows, (((1,), (1,)), ((), ())), preferred_element_type=jnp.float32
    )


def body(
    normed_block_input,
    stored_rotated_queries,
    stored_rotated_keys,
    attention_output_gradient,
    frozen_value_weight,
    adapter_down_weight,
    adapter_up_weight,
    packed_document_lengths,
):
    token_rows = normed_block_input.shape[1]
    model_features = normed_block_input.shape[2]
    hidden_activations = normed_block_input.reshape(token_rows, model_features)
    seq_count = lax.axis_size("seq")
    fsdp_count = lax.axis_size("fsdp")
    queries_per_group = QUERY_HEADS // KEY_VALUE_HEADS
    key_value_features = KEY_VALUE_HEADS * HEAD_FEATURES
    inverse = HEAD_FEATURES ** (-0.5)
    adapter_projection = contract_trailing(hidden_activations, adapter_down_weight)
    up_widened = adapter_up_weight.astype(jnp.float32)
    adapter_maps = ADAPTER_SCALE * jnp.dot(
        adapter_projection, up_widened, precision=lax.Precision.HIGHEST
    )
    base_value = jnp.dot(
        hidden_activations,
        lax.all_gather(frozen_value_weight, "fsdp", axis=0, tiled=True),
        preferred_element_type=jnp.float32,
    )
    adapter_values = (base_value + adapter_maps).astype(jnp.bfloat16)
    shaped = (token_rows, QUERY_HEADS, HEAD_FEATURES)
    key_broadcast = jnp.repeat(
        stored_rotated_keys.reshape(token_rows, KEY_VALUE_HEADS, HEAD_FEATURES),
        queries_per_group,
        axis=1,
    )
    value_broadcast = jnp.repeat(
        adapter_values.reshape(token_rows, KEY_VALUE_HEADS, HEAD_FEATURES),
        queries_per_group,
        axis=1,
    )
    head_query, head_key, head_value, head_grad = (
        lax.all_to_all(
            stored_rotated_queries.reshape(shaped), "seq", split_axis=1, concat_axis=0, tiled=True
        ),
        lax.all_to_all(key_broadcast, "seq", split_axis=1, concat_axis=0, tiled=True),
        lax.all_to_all(value_broadcast, "seq", split_axis=1, concat_axis=0, tiled=True),
        lax.all_to_all(
            attention_output_gradient.reshape(shaped),
            "seq",
            split_axis=1,
            concat_axis=0,
            tiled=True,
        ),
    )
    seq_len = head_query.shape[0]
    local_heads = head_query.shape[1]
    block_rows = min(512, seq_len)
    key_reach = block_rows + seq_len // 4
    bounds = jnp.cumsum(packed_document_lengths[0])
    places = jnp.arange(seq_len, dtype=jnp.int32)
    segments = jnp.sum((places[:, None] >= bounds[None, :]).astype(jnp.int32), axis=1)
    grad_keys = jnp.zeros((seq_len, local_heads, HEAD_FEATURES), jnp.float32)
    grad_values = jnp.zeros((seq_len, local_heads, HEAD_FEATURES), jnp.float32)
    query_parts = []
    for block_index in range(seq_len // block_rows):
        first_row = block_index * block_rows
        finish = first_row + block_rows
        opening = max(0, finish - key_reach)
        query_block = head_query[first_row:finish]
        grad_block = head_grad[first_row:finish]
        key_block = head_key[opening:finish]
        value_block = head_value[opening:finish]
        scores = (
            jnp.einsum("qhd,khd->hqk", query_block, key_block, preferred_element_type=jnp.float32)
            * inverse
        )
        allowed = (places[opening:finish][None, :] <= places[first_row:finish][:, None]) & (
            segments[opening:finish][None, :] == segments[first_row:finish][:, None]
        )
        scores = jnp.where(allowed[None], scores, NEG_FILL)
        row_peak = jnp.max(scores, axis=2, keepdims=True)
        weights = jnp.exp(scores - row_peak)
        probs_full = weights / jnp.sum(weights, axis=2, keepdims=True)
        probs_low = probs_full.astype(jnp.bfloat16)
        grad_probs = jnp.einsum(
            "qhd,khd->hqk", grad_block, value_block, preferred_element_type=jnp.float32
        )
        row_delta = jnp.sum(probs_full * grad_probs, axis=2, keepdims=True)
        grad_scores = (probs_full * (grad_probs - row_delta)).astype(jnp.bfloat16)
        query_parts.append(
            jnp.einsum("hqk,khd->qhd", grad_scores, key_block, preferred_element_type=jnp.float32)
            * inverse
        )
        key_part = (
            jnp.einsum("hqk,qhd->khd", grad_scores, query_block, preferred_element_type=jnp.float32)
            * inverse
        )
        value_part = jnp.einsum(
            "hqk,qhd->khd", probs_low, grad_block, preferred_element_type=jnp.float32
        )
        grad_keys = lax.dynamic_update_slice_in_dim(
            grad_keys, grad_keys[opening:finish] + key_part, opening, 0
        )
        grad_values = lax.dynamic_update_slice_in_dim(
            grad_values, grad_values[opening:finish] + value_part, opening, 0
        )
    grad_queries = jnp.concatenate(query_parts, axis=0).astype(jnp.bfloat16)
    token_query = lax.all_to_all(grad_queries, "seq", split_axis=0, concat_axis=1, tiled=True)
    rotated_query_gradient = token_query.reshape(1, token_rows, QUERY_HEADS * HEAD_FEATURES)
    token_key_matrix, token_value_matrix = (
        lax.all_to_all(grad_keys, "seq", split_axis=0, concat_axis=1, tiled=True),
        lax.all_to_all(grad_values, "seq", split_axis=0, concat_axis=1, tiled=True),
    )
    per_key_value_head = token_key_matrix.shape[1] // KEY_VALUE_HEADS
    rotated_key_gradient = (
        token_key_matrix.reshape(token_rows, KEY_VALUE_HEADS, per_key_value_head, HEAD_FEATURES)
        .sum(axis=2)
        .reshape(1, token_rows, key_value_features)
        .astype(jnp.bfloat16)
    )
    value_gradient_matrix = (
        token_value_matrix.reshape(token_rows, KEY_VALUE_HEADS, per_key_value_head, HEAD_FEATURES)
        .sum(axis=2)
        .reshape(token_rows, key_value_features)
    )
    value_grad_low = value_gradient_matrix.astype(jnp.bfloat16)
    adapter_rank_gradient = ADAPTER_SCALE * lax.dot_general(
        value_gradient_matrix, up_widened, (((1,), (1,)), ((), ())), precision=lax.Precision.HIGHEST
    )
    reduced_rank_gradient = adapter_rank_gradient.astype(jnp.bfloat16)
    frozen_path_gradient = contract_trailing(
        value_grad_low, lax.all_gather(frozen_value_weight, "fsdp", axis=0, tiled=True)
    )
    input_gradient = (
        frozen_path_gradient
        + jnp.dot(reduced_rank_gradient, adapter_down_weight, preferred_element_type=jnp.float32)
    ).astype(jnp.bfloat16)
    overall_token_count = token_rows * seq_count * fsdp_count
    down_shard = (
        lax.dot_general(
            reduced_rank_gradient,
            hidden_activations,
            (((0,), (0,)), ((), ())),
            preferred_element_type=jnp.float32,
        )
        / overall_token_count
    )
    up_shard = (
        ADAPTER_SCALE
        * jnp.dot(adapter_projection.T, value_gradient_matrix, precision=lax.Precision.HIGHEST)
        / overall_token_count
    )
    adapter_down_gradient, adapter_up_gradient = lax.psum((down_shard, up_shard), ("seq", "fsdp"))
    return (
        input_gradient.reshape(1, token_rows, model_features),
        rotated_query_gradient,
        rotated_key_gradient,
        adapter_down_gradient,
        adapter_up_gradient,
    )


def solution(mesh):
    placed = (
        P("fsdp", "seq", None),
        P("fsdp", "seq", None),
        P("fsdp", "seq", None),
        P("fsdp", "seq", None),
        P("fsdp", None),
        P(),
        P(),
        P("fsdp", None),
    )
    return jax.shard_map(
        body,
        mesh=mesh,
        in_specs=placed,
        out_specs=(
            P("fsdp", "seq", None),
            P("fsdp", "seq", None),
            P("fsdp", "seq", None),
            P(),
            P(),
        ),
        check_vma=False,
    )
```

profile of v0, /device:TPU:2, one launch (start us, length us, event | category | flops | bytes accessed | tf_op | source)
XLA Modules:
  0.0 526.1 jit_solution(7725692542050299921)
XLA Ops:
  11.0 7.6 %all-to-all-start.2 = ((bf16[128,32,128]{0,2,1:T(8,128)(2,1)}), bf16[128,32,128]{0,2,1:T(8,128)(2,1)S(1)}, u32[]{:S(2)}, u32[]{:S(2)}) async-start(bf16[128,32,128]{0,2,1:T(8,128)(2,1)} %bitcast.418), calls=%async_computation.2 | async-start | bytes 2097152 | tf_op jit(solution)/shard_map/all_to_all | solution.py:65
  20.5 14.2 %all-to-all-done.2 = bf16[128,32,128]{0,2,1:T(8,128)(2,1)S(1)} async-done(((bf16[128,32,128]{0,2,1:T(8,128)(2,1)}), bf16[128,32,128]{0,2,1:T(8,128)(2,1)S(1)}, u32[]{:S(2)}, u32[]{:S(2)}) %all-to-all-start.2) | async-done | bytes 1048608 | tf_op jit(solution)/shard_map/all_to_all | solution.py:65
  36.0 5.2 all-to-all-start.1
  49.0 8.3 %all-to-all-done.1 = bf16[128,32,128]{2,0,1:T(8,128)(2,1)S(1)} async-done(((bf16[128,32,128]{2,0,1:T(8,128)(2,1)}), bf16[128,32,128]{2,0,1:T(8,128)(2,1)S(1)}, u32[]{:S(2)}, u32[]{:S(2)}) %all-to-all-start.1) | async-done | bytes 1048608 | tf_op jit(solution)/shard_map/all_to_all | solution.py:63
  57.3 6.2 %all-to-all-start = ((bf16[128,32,128]{0,2,1:T(8,128)(2,1)}), bf16[128,32,128]{0,2,1:T(8,128)(2,1)}, u32[]{:S(2)}, u32[]{:S(2)}) async-start(bf16[128,32,128]{0,2,1:T(8,128)(2,1)} %bitcast.416), calls=%async_computation | async-start | bytes 2097152 | tf_op jit(solution)/shard_map/all_to_all | solution.py:60
  70.5 8.6 %all-to-all-done = bf16[128,32,128]{0,2,1:T(8,128)(2,1)} async-done(((bf16[128,32,128]{0,2,1:T(8,128)(2,1)}), bf16[128,32,128]{0,2,1:T(8,128)(2,1)}, u32[]{:S(2)}, u32[]{:S(2)}) %all-to-all-start) | async-done | bytes 1048608 | tf_op jit(solution)/shard_map/all_to_all | solution.py:60
  121.8 3.1 fusion.39
  124.9 3.1 fusion.41
  128.1 3.1 fusion.43
  131.2 3.1 fusion.45
  134.3 4.7 fusion.56
  140.6 5.1 all-to-all-start.4
  145.7 4.1 fusion.47
  149.8 3.1 fusion.49
  152.9 8.8 %all-to-all-done.4 = bf16[128,32,128]{2,0,1:T(8,128)(2,1)S(1)} async-done(((bf16[128,32,128]{2,0,1:T(8,128)(2,1)}), bf16[128,32,128]{2,0,1:T(8,128)(2,1)S(1)}, u32[]{:S(2)}, u32[]{:S(2)}) %all-to-all-start.4) | async-done | bytes 1048608 | tf_op jit(solution)/shard_map/all_to_all | solution.py:64
  161.8 5.8 %all-to-all-start.3 = ((f32[4096,1,128]{2,1,0:T(1,128)}), f32[4096,1,128]{2,1,0:T(1,128)}, u32[]{:S(2)}, u32[]{:S(2)}) async-start(f32[4096,1,128]{2,1,0:T(1,128)} %bitcast.62), calls=%async_computation.3 | async-start | bytes 4194304 | tf_op jit(solution)/shard_map/all_to_all | solution.py:130
  186.9 2.7 multiply_convert_fusion.5
  190.9 2.7 multiply_convert_fusion.4
  205.3 2.7 reduce.48
  213.5 2.6 fusion.37
  216.1 2.6 fusion.35
  218.8 7.8 %all-to-all-start.5 = ((bf16[32,2,8192]{2,1,0:T(2,128)(2,1)}), bf16[32,2,8192]{2,1,0:T(2,128)(2,1)S(1)}, u32[]{:S(2)}, u32[]{:S(2)}) async-start(bf16[32,2,8192]{2,1,0:T(2,128)(2,1)} %reshape.801), calls=%async_computation.5 | async-start | bytes 2097152 | tf_op jit(solution)/shard_map/all_to_all | solution.py:126
  226.6 3.3 fusion.33
  229.9 2.8 fusion.31
  232.8 2.7 fusion.29
  235.4 2.6 fusion.27
  238.1 4.4 all-to-all-done.5
  242.5 5.9 %all-to-all-start.6 = ((f32[4096,1,128]{2,1,0:T(1,128)}), f32[4096,1,128]{2,1,0:T(1,128)}, u32[]{:S(2)}, u32[]{:S(2)}) async-start(f32[4096,1,128]{2,1,0:T(1,128)} %bitcast.139), calls=%async_computation.6 | async-start | bytes 4194304 | tf_op jit(solution)/shard_map/all_to_all | solution.py:129
  253.7 90.2 %psum.15 = f32[16,512]{1,0:T(8,128)} all-reduce(f32[16,512]{1,0:T(8,128)S(1)} %convolution_multiply_fusion.25), channel_id=1, replica_groups=mesh['seq'=32,'fsdp'=8] {'seq','fsdp'}, use_global_device_ids=true, to_apply=%region_29.30 | all-reduce | flops 8192 | bytes 65536 | tf_op jit(solution)/shard_map/psum | solution.py:171
  344.0 6.3 %fusion.105 = f32[128,8192]{1,0:T(8,128)S(1)} fusion(bf16[8192,512]{1,0:T(8,128)(2,1)} %all-gather.2.cloned.1.call-done, f32[128,512]{0,1:T(8,128)S(1)} %bitcast.414), kind=kOutput, calls=%fused_computation.176 | convolution fusion | flops 1073807360 | bytes 12845056 | tf_op jit(solution)/shard_map/dot_general | solution.py:14
  352.3 3.4 reshape.802
  363.7 152.6 %all-reduce.4.cloned.1.call-done = f32[16,8192]{1,0:T(8,128)} async-done(((f32[16,8192]{1,0:T(8,128)}), f32[16,8192]{1,0:T(8,128)}) %all-reduce.4.cloned.1.call-update) | async-done | bytes 524304 | tf_op jit(solution)/shard_map/psum | solution.py:171
  (390 shorter events, 118.8 us)
Async XLA Ops:
  8.0 57.4 %copy-start = (bf16[1,128,8192]{2,1,0:T(8,128)(2,1)S(1)}, bf16[1,128,8192]{2,1,0:T(8,128)(2,1)}, u32[]{:S(2)}) copy-start(bf16[1,128,8192]{2,1,0:T(8,128)(2,1)} %param.8) | copy-start | bytes 6291460
  8.0 10.6 %copy-start.59 = (bf16[1,128,512]{2,1,0:T(8,128)(2,1)S(1)}, bf16[1,128,512]{2,1,0:T(8,128)(2,1)}, u32[]{:S(2)}) copy-start(bf16[1,128,512]{2,1,0:T(8,128)(2,1)} %param.10) | copy-start | bytes 393220
  8.0 126.3 %all-gather.2.cloned.1.call-start = ((), (), s32[]{:S(2)}) async-start(), calls=%async_computation.7 | async-start | bytes 9437184 | tf_op jit(solution)/shard_map/all_gather | solution.py:150
  11.0 23.6 %all-to-all-start.2 = ((bf16[128,32,128]{0,2,1:T(8,128)(2,1)}), bf16[128,32,128]{0,2,1:T(8,128)(2,1)S(1)}, u32[]{:S(2)}, u32[]{:S(2)}) async-start(bf16[128,32,128]{0,2,1:T(8,128)(2,1)} %bitcast.418), calls=%async_computation.2 | async-start | bytes 2097152 | tf_op jit(solution)/shard_map/all_to_all | solution.py:65
  18.7 25.3 %copy-start.135 = (s32[1,8]{1,0:T(1,128)S(1)}, s32[1,8]{1,0:T(1,128)}, u32[]{:S(2)}) copy-start(s32[1,8]{1,0:T(1,128)} %param.15) | copy-start | bytes 100
  36.0 29.4 %copy-start.34 = (bf16[16,8192]{1,0:T(8,128)(2,1)S(1)}, bf16[16,8192]{1,0:T(8,128)(2,1)}, u32[]{:S(2)}) copy-start(bf16[16,8192]{1,0:T(8,128)(2,1)} %param.13) | copy-start | bytes 786436
  36.0 21.3 %all-to-all-start.1 = ((bf16[128,32,128]{2,0,1:T(8,128)(2,1)}), bf16[128,32,128]{2,0,1:T(8,128)(2,1)S(1)}, u32[]{:S(2)}, u32[]{:S(2)}) async-start(bf16[128,32,128]{2,0,1:T(8,128)(2,1)} %bitcast.417), calls=%async_computation.1 | async-start | bytes 2097152 | tf_op jit(solution)/shard_map/all_to_all | solution.py:63
  49.0 19.8 %copy-start.44 = (s32[4096]{0:T(1024)}, s32[4096]{0:T(1024)S(1)}, u32[]{:S(2)}) copy-start(s32[4096]{0:T(1024)S(1)} %convert_reduce_fusion) | copy-start | bytes 49156
  57.3 21.9 %all-to-all-start = ((bf16[128,32,128]{0,2,1:T(8,128)(2,1)}), bf16[128,32,128]{0,2,1:T(8,128)(2,1)}, u32[]{:S(2)}, u32[]{:S(2)}) async-start(bf16[128,32,128]{0,2,1:T(8,128)(2,1)} %bitcast.416), calls=%async_computation | async-start | bytes 2097152 | tf_op jit(solution)/shard_map/all_to_all | solution.py:60
  68.9 32.8 %copy-start.126 = (s32[512]{0:T(512)S(1)}, s32[512]{0:T(512)}, u32[]{:S(2)}) copy-start(s32[512]{0:T(512)} %get-tuple-element.55) | copy-start | bytes 6148
  68.9 32.8 %copy-start.127 = (s32[512]{0:T(512)S(1)}, s32[512]{0:T(512)}, u32[]{:S(2)}) copy-start(s32[512]{0:T(512)} %get-tuple-element.94) | copy-start | bytes 6148
  107.0 13.1 %copy-start.14 = (f32[512,1024]{1,0:T(8,128)}, f32[512,1024]{1,0:T(8,128)S(1)}, u32[]{:S(2)}) copy-start(f32[512,1024]{1,0:T(8,128)S(1)} %get-tuple-element.65) | copy-start | bytes 6291460
  108.2 6.6 %copy-start.47 = (bf16[12,128,1,128]{3,1,0,2:T(8,128)(2,1)}, bf16[12,128,1,128]{3,1,0,2:T(8,128)(2,1)S(1)}, u32[]{:S(2)}) copy-start(bf16[12,128,1,128]{3,1,0,2:T(8,128)(2,1)S(1)} %get-tuple-element.27) | copy-start | bytes 1179652
  108.2 9.2 %copy-start.45 = (bf16[12,128,1,128]{3,1,0,2:T(8,128)(2,1)}, bf16[12,128,1,128]{3,1,0,2:T(8,128)(2,1)S(1)}, u32[]{:S(2)}) copy-start(bf16[12,128,1,128]{3,1,0,2:T(8,128)(2,1)S(1)} %get-tuple-element.26) | copy-start | bytes 1179652
  109.3 12.5 %copy-start.12 = (f32[512,1536]{1,0:T(8,128)}, f32[512,1536]{1,0:T(8,128)S(1)}, u32[]{:S(2)}) copy-start(f32[512,1536]{1,0:T(8,128)S(1)} %get-tuple-element.67) | copy-start | bytes 9437188
  109.3 12.5 %copy-start.105 = (f32[512]{0:T(512)}, f32[512]{0:T(512)S(1)}, u32[]{:S(2)}) copy-start(f32[512]{0:T(512)S(1)} %get-tuple-element.66) | copy-start | bytes 6148
  109.9 11.9 %copy-start.116 = (f32[512]{0:T(512)}, f32[512]{0:T(512)S(1)}, u32[]{:S(2)}) copy-start(f32[512]{0:T(512)S(1)} %fusion.9) | copy-start | bytes 6148
  110.9 14.0 %copy-start.10 = (f32[512,1536]{1,0:T(8,128)}, f32[512,1536]{1,0:T(8,128)S(1)}, u32[]{:S(2)}) copy-start(f32[512,1536]{1,0:T(8,128)S(1)} %get-tuple-element.69) | copy-start | bytes 9437188
  111.0 14.0 %copy-start.103 = (f32[512]{0:T(512)}, f32[512]{0:T(512)S(1)}, u32[]{:S(2)}) copy-start(f32[512]{0:T(512)S(1)} %get-tuple-element.68) | copy-start | bytes 6148
  111.5 13.4 %copy-start.114 = (f32[512]{0:T(512)}, f32[512]{0:T(512)S(1)}, u32[]{:S(2)}) copy-start(f32[512]{0:T(512)S(1)} %fusion.11) | copy-start | bytes 6148
  112.6 15.5 %copy-start.5 = (f32[512,1536]{1,0:T(8,128)}, f32[512,1536]{1,0:T(8,128)S(1)}, u32[]{:S(2)}) copy-start(f32[512,1536]{1,0:T(8,128)S(1)} %get-tuple-element.71) | copy-start | bytes 9437188
  112.6 15.5 %copy-start.98 = (f32[512]{0:T(512)}, f32[512]{0:T(512)S(1)}, u32[]{:S(2)}) copy-start(f32[512]{0:T(512)S(1)} %get-tuple-element.70) | copy-start | bytes 6148
  113.2 14.9 %copy-start.110 = (f32[512]{0:T(512)}, f32[512]{0:T(512)S(1)}, u32[]{:S(2)}) copy-start(f32[512]{0:T(512)S(1)} %fusion.13) | copy-start | bytes 6148
  114.2 17.0 %copy-start.3 = (f32[512,1536]{1,0:T(8,128)}, f32[512,1536]{1,0:T(8,128)S(1)}, u32[]{:S(2)}) copy-start(f32[512,1536]{1,0:T(8,128)S(1)} %get-tuple-element.73) | copy-start | bytes 9437188
  114.3 16.9 %copy-start.96 = (f32[512]{0:T(512)}, f32[512]{0:T(512)S(1)}, u32[]{:S(2)}) copy-start(f32[512]{0:T(512)S(1)} %get-tuple-element.72) | copy-start | bytes 6148
  114.8 16.4 %copy-start.108 = (f32[512]{0:T(512)}, f32[512]{0:T(512)S(1)}, u32[]{:S(2)}) copy-start(f32[512]{0:T(512)S(1)} %fusion.15) | copy-start | bytes 6148
  140.6 21.2 %all-to-all-start.4 = ((bf16[128,32,128]{2,0,1:T(8,128)(2,1)}), bf16[128,32,128]{2,0,1:T(8,128)(2,1)S(1)}, u32[]{:S(2)}, u32[]{:S(2)}) async-start(bf16[128,32,128]{2,0,1:T(8,128)(2,1)} %bitcast.419), calls=%async_computation.4 | async-start | bytes 2097152 | tf_op jit(solution)/shard_map/all_to_all | solution.py:64
  161.8 57.0 %all-to-all-start.3 = ((f32[4096,1,128]{2,1,0:T(1,128)}), f32[4096,1,128]{2,1,0:T(1,128)}, u32[]{:S(2)}, u32[]{:S(2)}) async-start(f32[4096,1,128]{2,1,0:T(1,128)} %bitcast.62), calls=%async_computation.3 | async-start | bytes 4194304 | tf_op jit(solution)/shard_map/all_to_all | solution.py:130
  218.8 23.7 %all-to-all-start.5 = ((bf16[32,2,8192]{2,1,0:T(2,128)(2,1)}), bf16[32,2,8192]{2,1,0:T(2,128)(2,1)S(1)}, u32[]{:S(2)}, u32[]{:S(2)}) async-start(bf16[32,2,8192]{2,1,0:T(2,128)(2,1)} %reshape.801), calls=%async_computation.5 | async-start | bytes 2097152 | tf_op jit(solution)/shard_map/all_to_all | solution.py:126
  242.5 9.5 %copy-start.77 = (bf16[16,512]{1,0:T(8,128)(2,1)S(1)}, bf16[16,512]{1,0:T(8,128)(2,1)}, u32[]{:S(2)}) copy-start(bf16[16,512]{1,0:T(8,128)(2,1)} %param.14) | copy-start | bytes 49156
  242.5 118.6 %all-to-all-start.6 = ((f32[4096,1,128]{2,1,0:T(1,128)}), f32[4096,1,128]{2,1,0:T(1,128)}, u32[]{:S(2)}, u32[]{:S(2)}) async-start(f32[4096,1,128]{2,1,0:T(1,128)} %bitcast.139), calls=%async_computation.6 | async-start | bytes 4194304 | tf_op jit(solution)/shard_map/all_to_all | solution.py:129
  248.4 267.9 %all-reduce.4.cloned.1.call-start = ((), (), s32[]{:S(2)}) async-start(), calls=%async_computation.8 | async-start | bytes 1048576 | tf_op jit(solution)/shard_map/psum | solution.py:171
  (114 other events, 279.3 us)
Sparse Core Ops, SparseCore 0:
  10.6 97.0 all-gather.1
Sparse Core Ops, SparseCore 1:
  255.0 261.3 all-reduce.3
where the time goes:
time: 530 us; the launch traced here: 526 us
  waiting for transfers between devices  198 us (37%)
  blocking collectives  90.2 us (17%)
  matrix products  86.9 us (16%)
  local copies, waits for them, and re-layouts  58.5 us (11%)
  starting transfers between devices  43.8 us (8%)
  other arithmetic  31.5 us (6%)
  between operations  17.6 us (3%)
    psum x1, waiting for transfers between devices, body(): lax.psum((down_shard, up_shard), ('seq', 'fsdp'))  153 us
    psum x1, blocking collectives, body(): lax.psum((down_shard, up_shard), ('seq', 'fsdp'))  90.2 us
    dot_general x8, matrix products, body(): jnp.einsum('hqk,qhd->khd', probs_low, grad_block, preferred_element_type=...  22.6 us
    unnamed x280, local copies, waits for them, and re-layouts  22.2 us
    dot_general x8, matrix products, body(): jnp.einsum('hqk,qhd->khd', grad_scores, query_block, preferred_element_ty...  19.5 us
    all_to_all x1, waiting for transfers between devices, body(): lax.all_to_all(attention_output_gradient.reshape(shaped), 'seq', split_ax...  14.2 us
    slice x9, local copies, waits for them, and re-layouts, body(): query_block = head_query[first_row:finish]  13.6 us
    slice x9, local copies, waits for them, and re-layouts, body(): grad_block = head_grad[first_row:finish]  11.4 us
  transfers between devices with their start and end apart: 9, of which 6 were waited for; matrix products, arithmetic and copies ran while one was open for 31% of the time, Pallas kernels for 0%

commit v1 on v0

--- a/solution.py
+++ b/solution.py
@@ -8,6 +8,7 @@
 KEY_VALUE_HEADS = 4
 ADAPTER_SCALE = 2.0
 NEG_FILL = -1e30
+fill_pairs_all_all = lambda work_x: lax.psum(lax.psum(work_x, "seq"), axis_name="fsdp")
 
 
 def contract_trailing(left_rows, right_rows):
@@ -168,7 +169,7 @@
         * jnp.dot(adapter_projection.T, value_gradient_matrix, precision=lax.Precision.HIGHEST)
         / overall_token_count
     )
-    adapter_down_gradient, adapter_up_gradient = lax.psum((down_shard, up_shard), ("seq", "fsdp"))
+    adapter_down_gradient, adapter_up_gradient = fill_pairs_all_all((down_shard, up_shard))
     return (
         input_gradient.reshape(1, token_rows, model_features),
         rotated_query_gradient,

time: 530 us -> 508 us (0.958)
  waiting for transfers between devices: 198 us -> 97.1 us
  blocking collectives: 90.2 us -> 168 us
    psum x1 -> x2, waiting for transfers between devices: 153 us -> 52.1 us  [the longest x1 52.1 us: lax.psum(lax.psum(work_x, 'seq'), axis_name='fsdp')]
    psum x1 -> x2, blocking collectives: 90.2 us -> 168 us  [the longest x1 134 us: lax.psum(work_x, 'seq')]
  transfers between devices with their start and end apart: 9 -> 10, of which waited for: 6 -> 6; matrix products, arithmetic and copies ran while one was open for 31% -> 32% of each run, Pallas kernels for 0% -> 0%
where the time goes in v1:
time: 508 us; the launch traced here: 503 us
  blocking collectives  168 us (33%)
  waiting for transfers between devices  97.1 us (19%)
  matrix products  86.9 us (17%)
  local copies, waits for them, and re-layouts  58.7 us (12%)
  starting transfers between devices  43.8 us (9%)
  other arithmetic  31.6 us (6%)
  between operations  17.6 us (3%)
    psum x1, blocking collectives, lax.psum(work_x, 'seq')  134 us
    psum x1, waiting for transfers between devices, lax.psum(lax.psum(work_x, 'seq'), axis_name='fsdp')  52.1 us
    psum x1, blocking collectives, lax.psum(lax.psum(work_x, 'seq'), axis_name='fsdp')  33.4 us
    dot_general x8, matrix products, body(): jnp.einsum('hqk,qhd->khd', probs_low, grad_block, preferred_element_type=...  22.6 us
    unnamed x280, local copies, waits for them, and re-layouts  22.3 us
    dot_general x8, matrix products, body(): jnp.einsum('hqk,qhd->khd', grad_scores, query_block, preferred_element_ty...  19.4 us
    all_to_all x1, waiting for transfers between devices, body(): lax.all_to_all(attention_output_gradient.reshape(shaped), 'seq', split_ax...  14.1 us
    slice x9, local copies, waits for them, and re-layouts, body(): query_block = head_query[first_row:finish]  13.6 us
  transfers between devices with their start and end apart: 10, of which 6 were waited for; matrix products, arithmetic and copies ran while one was open for 32% of the time, Pallas kernels for 0%

profile of v1, /device:TPU:2, one launch (start us, length us, event | category | flops | bytes accessed | tf_op | source)
XLA Modules:
  0.0 503.5 jit_solution(3713143607047965410)
XLA Ops:
  11.0 7.6 %all-to-all-start.2 = ((bf16[128,32,128]{0,2,1:T(8,128)(2,1)}), bf16[128,32,128]{0,2,1:T(8,128)(2,1)S(1)}, u32[]{:S(2)}, u32[]{:S(2)}) async-start(bf16[128,32,128]{0,2,1:T(8,128)(2,1)} %bitcast.418), calls=%async_computation.2 | async-start | bytes 2097152 | tf_op jit(solution)/shard_map/all_to_all | solution.py:66
  20.5 14.1 %all-to-all-done.2 = bf16[128,32,128]{0,2,1:T(8,128)(2,1)S(1)} async-done(((bf16[128,32,128]{0,2,1:T(8,128)(2,1)}), bf16[128,32,128]{0,2,1:T(8,128)(2,1)S(1)}, u32[]{:S(2)}, u32[]{:S(2)}) %all-to-all-start.2) | async-done | bytes 1048608 | tf_op jit(solution)/shard_map/all_to_all | solution.py:66
  36.0 5.2 %all-to-all-start.1 = ((bf16[128,32,128]{2,0,1:T(8,128)(2,1)}), bf16[128,32,128]{2,0,1:T(8,128)(2,1)S(1)}, u32[]{:S(2)}, u32[]{:S(2)}) async-start(bf16[128,32,128]{2,0,1:T(8,128)(2,1)} %bitcast.417), calls=%async_computation.1 | async-start | bytes 2097152 | tf_op jit(solution)/shard_map/all_to_all | solution.py:64
  49.1 8.2 %all-to-all-done.1 = bf16[128,32,128]{2,0,1:T(8,128)(2,1)S(1)} async-done(((bf16[128,32,128]{2,0,1:T(8,128)(2,1)}), bf16[128,32,128]{2,0,1:T(8,128)(2,1)S(1)}, u32[]{:S(2)}, u32[]{:S(2)}) %all-to-all-start.1) | async-done | bytes 1048608 | tf_op jit(solution)/shard_map/all_to_all | solution.py:64
  57.3 6.2 %all-to-all-start = ((bf16[128,32,128]{0,2,1:T(8,128)(2,1)}), bf16[128,32,128]{0,2,1:T(8,128)(2,1)}, u32[]{:S(2)}, u32[]{:S(2)}) async-start(bf16[128,32,128]{0,2,1:T(8,128)(2,1)} %bitcast.416), calls=%async_computation | async-start | bytes 2097152 | tf_op jit(solution)/shard_map/all_to_all | solution.py:61
  70.5 8.6 %all-to-all-done = bf16[128,32,128]{0,2,1:T(8,128)(2,1)} async-done(((bf16[128,32,128]{0,2,1:T(8,128)(2,1)}), bf16[128,32,128]{0,2,1:T(8,128)(2,1)}, u32[]{:S(2)}, u32[]{:S(2)}) %all-to-all-start) | async-done | bytes 1048608 | tf_op jit(solution)/shard_map/all_to_all | solution.py:61
  121.9 3.1 fusion.39
  125.0 3.1 fusion.41
  128.2 3.1 fusion.43
  131.3 3.1 fusion.45
  134.4 4.7 fusion.56
  140.7 5.1 %all-to-all-start.4 = ((bf16[128,32,128]{2,0,1:T(8,128)(2,1)}), bf16[128,32,128]{2,0,1:T(8,128)(2,1)S(1)}, u32[]{:S(2)}, u32[]{:S(2)}) async-start(bf16[128,32,128]{2,0,1:T(8,128)(2,1)} %bitcast.419), calls=%async_computation.4 | async-start | bytes 2097152 | tf_op jit(solution)/shard_map/all_to_all | solution.py:65
  145.8 4.1 fusion.47
  149.9 3.1 fusion.49
  153.0 8.8 %all-to-all-done.4 = bf16[128,32,128]{2,0,1:T(8,128)(2,1)S(1)} async-done(((bf16[128,32,128]{2,0,1:T(8,128)(2,1)}), bf16[128,32,128]{2,0,1:T(8,128)(2,1)S(1)}, u32[]{:S(2)}, u32[]{:S(2)}) %all-to-all-start.4) | async-done | bytes 1048608 | tf_op jit(solution)/shard_map/all_to_all | solution.py:65
  161.9 5.8 %all-to-all-start.3 = ((f32[4096,1,128]{2,1,0:T(1,128)}), f32[4096,1,128]{2,1,0:T(1,128)}, u32[]{:S(2)}, u32[]{:S(2)}) async-start(f32[4096,1,128]{2,1,0:T(1,128)} %bitcast.62), calls=%async_computation.3 | async-start | bytes 4194304 | tf_op jit(solution)/shard_map/all_to_all | solution.py:131
  187.1 2.7 multiply_convert_fusion.5
  191.1 2.7 multiply_convert_fusion.4
  205.5 2.7 reduce.48
  213.6 2.6 fusion.37
  218.9 7.8 %all-to-all-start.5 = ((bf16[32,2,8192]{2,1,0:T(2,128)(2,1)}), bf16[32,2,8192]{2,1,0:T(2,128)(2,1)S(1)}, u32[]{:S(2)}, u32[]{:S(2)}) async-start(bf16[32,2,8192]{2,1,0:T(2,128)(2,1)} %reshape.801), calls=%async_computation.5 | async-start | bytes 2097152 | tf_op jit(solution)/shard_map/all_to_all | solution.py:127
  226.8 3.3 fusion.33
  230.1 2.8 fusion.31
  232.9 2.7 fusion.29
  235.6 2.7 fusion.27
  238.2 4.4 all-to-all-done.5
  242.6 6.0 %all-to-all-start.6 = ((f32[4096,1,128]{2,1,0:T(1,128)}), f32[4096,1,128]{2,1,0:T(1,128)}, u32[]{:S(2)}, u32[]{:S(2)}) async-start(f32[4096,1,128]{2,1,0:T(1,128)} %bitcast.139), calls=%async_computation.6 | async-start | bytes 4194304 | tf_op jit(solution)/shard_map/all_to_all | solution.py:130
  253.9 134.4 %psum.30 = f32[16,512]{1,0:T(8,128)S(1)} all-reduce(f32[16,512]{1,0:T(8,128)S(1)} %convolution_multiply_fusion.25), channel_id=1, replica_groups=mesh['seq'=32,'fsdp'=8] {'seq'}, use_global_device_ids=true, to_apply=%region_30.31 | all-reduce | flops 8192 | bytes 65536 | tf_op jit(solution)/shard_map/psum | solution.py:11
  388.4 33.4 %psum.31 = f32[16,512]{1,0:T(8,128)} all-reduce(f32[16,512]{1,0:T(8,128)S(1)} %psum.30), channel_id=1, replica_groups=mesh['seq'=32,'fsdp'=8] {'fsdp'}, use_global_device_ids=true, to_apply=%region_31.32 | all-reduce | flops 8192 | bytes 65536 | tf_op jit(solution)/shard_map/psum | solution.py:11
  421.8 6.3 %fusion.105 = f32[128,8192]{1,0:T(8,128)S(1)} fusion(bf16[8192,512]{1,0:T(8,128)(2,1)} %all-gather.2.cloned.1.call-done, f32[128,512]{0,1:T(8,128)S(1)} %bitcast.414), kind=kOutput, calls=%fused_computation.176 | convolution fusion | flops 1073807360 | bytes 12845056 | tf_op jit(solution)/shard_map/dot_general | solution.py:15
  430.1 3.4 reshape.802
  441.6 52.1 %all-reduce.7.cloned.1.call-done = f32[16,8192]{1,0:T(8,128)} async-done(((f32[16,8192]{1,0:T(8,128)}), f32[16,8192]{1,0:T(8,128)}) %all-reduce.7.cloned.1.call-update) | async-done | bytes 524304 | tf_op jit(solution)/shard_map/psum | solution.py:11
  (394 shorter events, 121.9 us)
Async XLA Ops:
  8.0 57.4 %copy-start = (bf16[1,128,8192]{2,1,0:T(8,128)(2,1)S(1)}, bf16[1,128,8192]{2,1,0:T(8,128)(2,1)}, u32[]{:S(2)}) copy-start(bf16[1,128,8192]{2,1,0:T(8,128)(2,1)} %param.8) | copy-start | bytes 6291460
  8.0 10.6 %copy-start.59 = (bf16[1,128,512]{2,1,0:T(8,128)(2,1)S(1)}, bf16[1,128,512]{2,1,0:T(8,128)(2,1)}, u32[]{:S(2)}) copy-start(bf16[1,128,512]{2,1,0:T(8,128)(2,1)} %param.10) | copy-start | bytes 393220
  8.0 126.4 %all-gather.2.cloned.1.call-start = ((), (), s32[]{:S(2)}) async-start(), calls=%async_computation.7 | async-start | bytes 9437184 | tf_op jit(solution)/shard_map/all_gather | solution.py:151
  11.0 23.6 %all-to-all-start.2 = ((bf16[128,32,128]{0,2,1:T(8,128)(2,1)}), bf16[128,32,128]{0,2,1:T(8,128)(2,1)S(1)}, u32[]{:S(2)}, u32[]{:S(2)}) async-start(bf16[128,32,128]{0,2,1:T(8,128)(2,1)} %bitcast.418), calls=%async_computation.2 | async-start | bytes 2097152 | tf_op jit(solution)/shard_map/all_to_all | solution.py:66
  18.7 25.4 %copy-start.135 = (s32[1,8]{1,0:T(1,128)S(1)}, s32[1,8]{1,0:T(1,128)}, u32[]{:S(2)}) copy-start(s32[1,8]{1,0:T(1,128)} %param.15) | copy-start | bytes 100
  36.0 29.4 %copy-start.34 = (bf16[16,8192]{1,0:T(8,128)(2,1)S(1)}, bf16[16,8192]{1,0:T(8,128)(2,1)}, u32[]{:S(2)}) copy-start(bf16[16,8192]{1,0:T(8,128)(2,1)} %param.13) | copy-start | bytes 786436
  36.0 21.3 %all-to-all-start.1 = ((bf16[128,32,128]{2,0,1:T(8,128)(2,1)}), bf16[128,32,128]{2,0,1:T(8,128)(2,1)S(1)}, u32[]{:S(2)}, u32[]{:S(2)}) async-start(bf16[128,32,128]{2,0,1:T(8,128)(2,1)} %bitcast.417), calls=%async_computation.1 | async-start | bytes 2097152 | tf_op jit(solution)/shard_map/all_to_all | solution.py:64
  49.1 19.8 %copy-start.44 = (s32[4096]{0:T(1024)}, s32[4096]{0:T(1024)S(1)}, u32[]{:S(2)}) copy-start(s32[4096]{0:T(1024)S(1)} %convert_reduce_fusion) | copy-start | bytes 49156
  57.3 21.9 %all-to-all-start = ((bf16[128,32,128]{0,2,1:T(8,128)(2,1)}), bf16[128,32,128]{0,2,1:T(8,128)(2,1)}, u32[]{:S(2)}, u32[]{:S(2)}) async-start(bf16[128,32,128]{0,2,1:T(8,128)(2,1)} %bitcast.416), calls=%async_computation | async-start | bytes 2097152 | tf_op jit(solution)/shard_map/all_to_all | solution.py:61
  68.9 32.9 %copy-start.126 = (s32[512]{0:T(512)S(1)}, s32[512]{0:T(512)}, u32[]{:S(2)}) copy-start(s32[512]{0:T(512)} %get-tuple-element.55) | copy-start | bytes 6148
  68.9 32.9 %copy-start.127 = (s32[512]{0:T(512)S(1)}, s32[512]{0:T(512)}, u32[]{:S(2)}) copy-start(s32[512]{0:T(512)} %get-tuple-element.94) | copy-start | bytes 6148
  107.1 13.2 %copy-start.14 = (f32[512,1024]{1,0:T(8,128)}, f32[512,1024]{1,0:T(8,128)S(1)}, u32[]{:S(2)}) copy-start(f32[512,1024]{1,0:T(8,128)S(1)} %get-tuple-element.65) | copy-start | bytes 6291460
  108.3 9.2 %copy-start.45 = (bf16[12,128,1,128]{3,1,0,2:T(8,128)(2,1)}, bf16[12,128,1,128]{3,1,0,2:T(8,128)(2,1)S(1)}, u32[]{:S(2)}) copy-start(bf16[12,128,1,128]{3,1,0,2:T(8,128)(2,1)S(1)} %get-tuple-element.26) | copy-start | bytes 1179652
  109.3 12.5 %copy-start.12 = (f32[512,1536]{1,0:T(8,128)}, f32[512,1536]{1,0:T(8,128)S(1)}, u32[]{:S(2)}) copy-start(f32[512,1536]{1,0:T(8,128)S(1)} %get-tuple-element.67) | copy-start | bytes 9437188
  109.3 12.5 %copy-start.105 = (f32[512]{0:T(512)}, f32[512]{0:T(512)S(1)}, u32[]{:S(2)}) copy-start(f32[512]{0:T(512)S(1)} %get-tuple-element.66) | copy-start | bytes 6148
  109.9 11.9 %copy-start.116 = (f32[512]{0:T(512)}, f32[512]{0:T(512)S(1)}, u32[]{:S(2)}) copy-start(f32[512]{0:T(512)S(1)} %fusion.9) | copy-start | bytes 6148
  111.0 14.0 %copy-start.10 = (f32[512,1536]{1,0:T(8,128)}, f32[512,1536]{1,0:T(8,128)S(1)}, u32[]{:S(2)}) copy-start(f32[512,1536]{1,0:T(8,128)S(1)} %get-tuple-element.69) | copy-start | bytes 9437188
  111.0 14.0 %copy-start.103 = (f32[512]{0:T(512)}, f32[512]{0:T(512)S(1)}, u32[]{:S(2)}) copy-start(f32[512]{0:T(512)S(1)} %get-tuple-element.68) | copy-start | bytes 6148
  111.6 13.4 %copy-start.114 = (f32[512]{0:T(512)}, f32[512]{0:T(512)S(1)}, u32[]{:S(2)}) copy-start(f32[512]{0:T(512)S(1)} %fusion.11) | copy-start | bytes 6148
  112.7 15.5 %copy-start.5 = (f32[512,1536]{1,0:T(8,128)}, f32[512,1536]{1,0:T(8,128)S(1)}, u32[]{:S(2)}) copy-start(f32[512,1536]{1,0:T(8,128)S(1)} %get-tuple-element.71) | copy-start | bytes 9437188
  112.7 15.5 %copy-start.98 = (f32[512]{0:T(512)}, f32[512]{0:T(512)S(1)}, u32[]{:S(2)}) copy-start(f32[512]{0:T(512)S(1)} %get-tuple-element.70) | copy-start | bytes 6148
  113.2 14.9 %copy-start.110 = (f32[512]{0:T(512)}, f32[512]{0:T(512)S(1)}, u32[]{:S(2)}) copy-start(f32[512]{0:T(512)S(1)} %fusion.13) | copy-start | bytes 6148
  114.3 17.0 %copy-start.3 = (f32[512,1536]{1,0:T(8,128)}, f32[512,1536]{1,0:T(8,128)S(1)}, u32[]{:S(2)}) copy-start(f32[512,1536]{1,0:T(8,128)S(1)} %get-tuple-element.73) | copy-start | bytes 9437188
  114.3 17.0 %copy-start.96 = (f32[512]{0:T(512)}, f32[512]{0:T(512)S(1)}, u32[]{:S(2)}) copy-start(f32[512]{0:T(512)S(1)} %get-tuple-element.72) | copy-start | bytes 6148
  114.9 16.4 %copy-start.108 = (f32[512]{0:T(512)}, f32[512]{0:T(512)S(1)}, u32[]{:S(2)}) copy-start(f32[512]{0:T(512)S(1)} %fusion.15) | copy-start | bytes 6148
  140.7 21.2 %all-to-all-start.4 = ((bf16[128,32,128]{2,0,1:T(8,128)(2,1)}), bf16[128,32,128]{2,0,1:T(8,128)(2,1)S(1)}, u32[]{:S(2)}, u32[]{:S(2)}) async-start(bf16[128,32,128]{2,0,1:T(8,128)(2,1)} %bitcast.419), calls=%async_computation.4 | async-start | bytes 2097152 | tf_op jit(solution)/shard_map/all_to_all | solution.py:65
  161.9 57.1 %all-to-all-start.3 = ((f32[4096,1,128]{2,1,0:T(1,128)}), f32[4096,1,128]{2,1,0:T(1,128)}, u32[]{:S(2)}, u32[]{:S(2)}) async-start(f32[4096,1,128]{2,1,0:T(1,128)} %bitcast.62), calls=%async_computation.3 | async-start | bytes 4194304 | tf_op jit(solution)/shard_map/all_to_all | solution.py:131
  218.9 23.7 %all-to-all-start.5 = ((bf16[32,2,8192]{2,1,0:T(2,128)(2,1)}), bf16[32,2,8192]{2,1,0:T(2,128)(2,1)S(1)}, u32[]{:S(2)}, u32[]{:S(2)}) async-start(bf16[32,2,8192]{2,1,0:T(2,128)(2,1)} %reshape.801), calls=%async_computation.5 | async-start | bytes 2097152 | tf_op jit(solution)/shard_map/all_to_all | solution.py:127
  242.6 9.5 %copy-start.77 = (bf16[16,512]{1,0:T(8,128)(2,1)S(1)}, bf16[16,512]{1,0:T(8,128)(2,1)}, u32[]{:S(2)}) copy-start(bf16[16,512]{1,0:T(8,128)(2,1)} %param.14) | copy-start | bytes 49156
  242.6 196.3 %all-to-all-start.6 = ((f32[4096,1,128]{2,1,0:T(1,128)}), f32[4096,1,128]{2,1,0:T(1,128)}, u32[]{:S(2)}, u32[]{:S(2)}) async-start(f32[4096,1,128]{2,1,0:T(1,128)} %bitcast.139), calls=%async_computation.6 | async-start | bytes 4194304 | tf_op jit(solution)/shard_map/all_to_all | solution.py:130
  248.6 173.2 %all-reduce.5.cloned.1.call-start = ((), (), s32[]{:S(2)}) async-start(), calls=%async_computation.8 | async-start | bytes 1048576 | tf_op jit(solution)/shard_map/psum | solution.py:11
  253.6 240.1 %all-reduce.7.cloned.1.call-start = ((), (), s32[]{:S(2)}) async-start(), calls=%async_computation.9 | async-start | bytes 1048576 | tf_op jit(solution)/shard_map/psum | solution.py:11
  (115 other events, 286.2 us)
Sparse Core Ops, SparseCore 0:
  10.6 97.0 all-gather.1
  421.9 71.7 all-reduce.6
Sparse Core Ops, SparseCore 1:
  253.7 121.8 all-reduce.4
